TPU v7x, 256 devices: a whole 4x4x8 slice. The times are simulated.
256 devices in a mesh: group: 32 (over x, y, core), tp: 8 (over z).
Axes of the slice: x: 4, y: 4, z: 8, core: 2. Of those that a mesh axis runs over, the one named last changes fastest.
Arguments:
- hidden_in: bfloat16 [64, 3072], P('group'), may hold values from -6 to 6
- w_qkv: bfloat16 [3072, 2048], P(None, 'tp'), may hold values from -0.109375 to 0.109375
- w_out: bfloat16 [1536, 3072], P('tp'), may hold values from -0.15625 to 0.15625
- kv_pool: bfloat16 [2048, 128, 512], P(('group', 'tp'))
- page_table: int32 [64, 32], replicated, may hold values from 0 to 2047, as said below
- lengths: int32 [64], replicated, may hold values from 1 to 4096, as said below
Outputs:
- attn_proj: bfloat16 [64, 3072], P('group', 'tp')
Inputs may be any that keep to these rules, and one draw needn't show every extreme that they name: `page_table`: every pool slot is named by exactly one request page. `lengths`: some request has the full 32 * 128 cached tokens.
All inputs are finite; a program needn't handle non-finite values.
Results may differ from a plain program's by a relative error of at most 0.0085.
The roundings to bfloat16 on the way count: a program that leaves them out, or rounds other values in their place, can miss the bound.
Values may be sent and summed in bfloat16 or wider, within the bound.
A program may use at most 64 MiB of HBM per device.

v0:
```python
import jax
import jax.numpy as jnp
from jax import lax
from jax.sharding import PartitionSpec as P

HEADS = 12
KV_HEADS = 2
HEAD_DIM = 128


def on_device(hidden_in, w_qkv, w_out, kv_pool, page_table, lengths):
    qdim = HEADS * HEAD_DIM
    kdim = KV_HEADS * HEAD_DIM
    per_kv = HEADS // KV_HEADS
    scale = HEAD_DIM ** (-0.5)
    req_grp = hidden_in.shape[0]
    col_count = w_out.shape[0]
    col_start = lax.axis_index("tp") * col_count
    columns = jnp.dot(hidden_in, w_qkv, preferred_element_type=jnp.float32).astype(jnp.bfloat16)
    qkv = lax.all_gather(columns, "tp", axis=1, tiled=True)
    queries = lax.all_gather(qkv[:, :qdim], "group", axis=0, tiled=True)
    requests = queries.shape[0]
    slot_count = kv_pool.shape[0]
    page_len = kv_pool.shape[1]
    max_pages = page_table.shape[1]
    slot_ids = lax.axis_index(("group", "tp")) * slot_count + jnp.arange(
        slot_count, dtype=jnp.int32
    )
    match = page_table[:, :, None] == slot_ids[None, None, :]
    slot_req = jnp.sum(
        jnp.where(match, jnp.arange(requests, dtype=jnp.int32)[:, None, None], 0), axis=(0, 1)
    )
    slot_page = jnp.sum(
        jnp.where(match, jnp.arange(max_pages, dtype=jnp.int32)[None, :, None], 0), axis=(0, 1)
    )
    chosen = queries[slot_req].reshape(slot_count, KV_HEADS, per_kv, HEAD_DIM)
    keys = kv_pool[..., :kdim].reshape(slot_count, page_len, KV_HEADS, HEAD_DIM)
    values = kv_pool[..., kdim:].reshape(slot_count, page_len, KV_HEADS, HEAD_DIM)
    scores = jnp.einsum("pgjd,ptgd->pgjt", chosen, keys, preferred_element_type=jnp.float32) * scale
    position = slot_page[:, None] * page_len + jnp.arange(page_len, dtype=jnp.int32)[None, :]
    live = (position < lengths[slot_req][:, None])[:, None, None, :]
    top = jnp.max(jnp.where(live, scores, -1e30), axis=-1)
    probs = jnp.where(live, jnp.exp(scores - top[..., None]), 0.0).astype(jnp.bfloat16)
    total = jnp.sum(probs.astype(jnp.float32), axis=-1)
    weighted = jnp.einsum("pgjt,ptgd->pgjd", probs, values, preferred_element_type=jnp.float32)
    owner = slot_req[None, :] == jnp.arange(requests, dtype=jnp.int32)[:, None]
    req_top = jnp.max(jnp.where(owner[:, :, None, None], top[None], -1e30), axis=1)
    factor = jnp.exp(top - req_top[slot_req])
    onehot = owner.astype(jnp.float32)
    req_total = jnp.einsum(
        "rp,pgj->rgj", onehot, total * factor, precision=lax.Precision.HIGHEST
    ).reshape(requests, HEADS)
    req_sums = jnp.einsum(
        "rp,pgjd->rgjd", onehot, weighted * factor[..., None], precision=lax.Precision.HIGHEST
    ).reshape(requests, qdim)
    req_top = req_top.reshape(requests, HEADS)
    start = lax.axis_index("group") * req_grp
    peak_all = lax.pmax(req_top, ("group", "tp"))
    rescale = jnp.exp(req_top - peak_all)
    total_all, sums_all = lax.psum(
        (req_total * rescale, req_sums * jnp.repeat(rescale, HEAD_DIM, axis=1)), ("group", "tp")
    )
    peak = lax.dynamic_slice_in_dim(peak_all, start, req_grp, 0)
    whole = lax.dynamic_slice_in_dim(total_all, start, req_grp, 0)
    sums = lax.dynamic_slice_in_dim(sums_all, start, req_grp, 0)
    sums_part = lax.dynamic_slice_in_dim(sums, col_start, col_count, 1)
    own_q = qkv[:, :qdim].reshape(req_grp, KV_HEADS, per_kv, HEAD_DIM)
    own_k = qkv[:, qdim : qdim + kdim].reshape(req_grp, KV_HEADS, HEAD_DIM)
    own_v = qkv[:, qdim + kdim :].reshape(req_grp, KV_HEADS, HEAD_DIM)
    own_score = (
        jnp.einsum("rgjd,rgd->rgj", own_q, own_k, preferred_element_type=jnp.float32) * scale
    ).reshape(req_grp, HEADS)
    own_sums = jnp.broadcast_to(
        own_v.astype(jnp.float32)[:, :, None, :], (req_grp, KV_HEADS, per_kv, HEAD_DIM)
    ).reshape(req_grp, qdim)
    new_peak = jnp.maximum(peak, own_score)
    old_factor = jnp.exp(peak - new_peak)
    own_factor = jnp.exp(own_score - new_peak)
    new_whole = whole * old_factor + own_factor

    def pick(values_full):
        return lax.dynamic_slice_in_dim(values_full, col_start, col_count, 1)

    new_sums = sums_part * pick(jnp.repeat(old_factor, HEAD_DIM, axis=1)) + pick(
        own_sums * jnp.repeat(own_factor, HEAD_DIM, axis=1)
    )
    attn_part = (new_sums / pick(jnp.repeat(new_whole, HEAD_DIM, axis=1))).astype(jnp.bfloat16)
    partial_value = jnp.dot(attn_part, w_out, preferred_element_type=jnp.float32)
    return lax.psum_scatter(partial_value, "tp", scatter_dimension=1, tiled=True).astype(
        jnp.bfloat16
    )


def solution(mesh):
    in_specs = (
        P("group", None),
        P(None, "tp"),
        P("tp", None),
        P(("group", "tp"), None, None),
        P(),
        P(),
    )
    out_specs = P("group", "tp")
    return jax.shard_map(
        on_device, mesh=mesh, in_specs=in_specs, out_specs=out_specs, check_vma=False
    )
```

profile of v0, /device:TPU:1, one launch (start us, length us, event | category | flops | bytes accessed | tf_op | source)
XLA Modules:
  0.0 425.9 jit_solution(9588263399593622062)
XLA Ops:
  6.5 1.1 fusion.1
  7.7 0.2 copy-done
  8.0 1.0 convolution_convert_fusion
  9.0 16.5 %all_gather.6 = bf16[2,2048]{1,0:T(2,128)(2,1)S(1)} all-gather(bf16[2,256]{1,0:T(2,128)(2,1)S(1)} %convolution_convert_fusion), channel_id=1, replica_groups=mesh['group'=32,'tp'=8] {'tp'}, dimensions={1}, use_global_device_ids=true | all-gather | bytes 9216 | tf_op jit(solution)/shard_map/all_gather | solution.py:20
  25.5 29.0 %all-gather = bf16[32,2,1536]{2,1,0:T(2,128)(2,1)S(1)} all-gather(bf16[1,2,1536]{2,1,0:T(2,128)(2,1)S(1)} %get-tuple-element.19), channel_id=1, replica_groups=mesh['group'=32,'tp'=8] {'group'}, dimensions={0}, use_global_device_ids=true | all-gather | bytes 202752 | tf_op jit(solution)/shard_map/all_gather | solution.py:21
  54.6 0.6 gather_fusion
  55.2 0.6 gather_fusion.1
  55.8 1.3 fusion.25
  57.1 0.3 copy.96
  57.4 0.3 select_reduce_fusion
  58.1 0.3 copy.97
  58.4 0.2 convert_reduce_fusion
  58.7 73.4 %pmax.7 = f32[64,12]{1,0:T(8,128)S(1)} all-reduce(f32[64,12]{1,0:T(8,128)S(1)} %copy.86), channel_id=1, replica_groups=mesh['group'=32,'tp'=8] {'group','tp'}, use_global_device_ids=true, to_apply=%region_4.5 | all-reduce | flops 768 | bytes 6144 | tf_op jit(solution)/shard_map/pmax | solution.py:58
  132.0 0.6 gather_fusion.2
  132.9 0.4 convolution_multiply_fusion
  133.4 0.4 fusion.2
  133.8 0.2 copy.84
  134.2 0.2 broadcast_in_dim.104
  134.4 0.9 bitcast_multiply_fusion
  135.7 74.9 %psum.15 = f32[64,12]{1,0:T(8,128)S(1)} all-reduce(f32[64,12]{1,0:T(8,128)S(1)} %get-tuple-element.10), channel_id=1, replica_groups=mesh['group'=32,'tp'=8] {'group','tp'}, use_global_device_ids=true, to_apply=%region_7.8 | all-reduce | flops 768 | bytes 6144 | tf_op jit(solution)/shard_map/psum | solution.py:60
  210.8 168.7 %all-reduce.2.cloned.1.call-done = f32[64,1536]{1,0:T(8,128)} async-done(((f32[64,1536]{1,0:T(8,128)}), f32[64,1536]{1,0:T(8,128)}) %all-reduce.2.cloned.1.call-update) | async-done | bytes 393232 | tf_op jit(solution)/shard_map/psum | solution.py:60
  379.5 2.7 convolution_bitcast_fusion
  382.2 35.2 %reduce-scatter.4.cloned.1.call-done = f32[384,2]{1,0:T(8,128)} async-done(((f32[3072,2]{1,0:T(8,128)}), f32[384,2]{1,0:T(8,128)}) %reduce-scatter.4.cloned.1.call-update) | async-done | bytes 3088
  417.4 1.6 copy.95
  (43 shorter events, 1.6 us)
Async XLA Ops:
  6.5 1.4 copy-start
  6.5 48.0 %copy-start.1 = (s32[64]{0:T(128)S(1)}, s32[64]{0:T(128)}, u32[]{:S(2)}) copy-start(s32[64]{0:T(128)} %param.11) | copy-start | bytes 772
  6.5 372.9 %all-reduce.2.cloned.1.call-start = ((), (), s32[]{:S(2)}) async-start(), calls=%async_computation.1 | async-start | bytes 786432 | tf_op jit(solution)/shard_map/psum | solution.py:60
  134.2 245.3 %copy-start.2 = (bf16[192,3072]{1,0:T(8,128)(2,1)S(1)}, bf16[192,3072]{1,0:T(8,128)(2,1)}, u32[]{:S(2)}) copy-start(bf16[192,3072]{1,0:T(8,128)(2,1)} %param.8) | copy-start | bytes 3538948
  135.3 282.1 %reduce-scatter.4.cloned.1.call-start = ((), (), s32[]{:S(2)}) async-start(), calls=%async_computation.2 | async-start | bytes 1769472
Sparse Core Ops, SparseCore 0:
  135.4 243.9 all-reduce.1
  382.3 35.0 reduce-scatter.3
where the time goes:
time: 430 us; the launch traced here: 426 us
  waiting for transfers between devices  204 us (47%)
  blocking collectives  194 us (45%)
  between operations  13.6 us (3%)
  local copies, waits for them, and re-layouts  6.81 us (2%)
  matrix products  5.2 us (1%)
    psum x1, waiting for transfers between devices, on_device(): lax.psum((req_total * rescale, req_sums * jnp.repeat(rescale, HEAD_DIM, a...  169 us
    psum x1, blocking collectives, on_device(): lax.psum((req_total * rescale, req_sums * jnp.repeat(rescale, HEAD_DIM, a...  74.9 us
    pmax x1, blocking collectives, on_device(): peak_all = lax.pmax(req_top, ('group', 'tp'))  73.4 us
    unnamed x3, waiting for transfers between devices  35.3 us
    all_gather x1, blocking collectives, on_device(): queries = lax.all_gather(qkv[:, :qdim], 'group', axis=0, tiled=True)  29 us
    all_gather x1, blocking collectives, on_device(): qkv = lax.all_gather(columns, 'tp', axis=1, tiled=True)  16.5 us
  transfers between devices with their start and end apart: 2, of which 2 were waited for; matrix products, arithmetic and copies ran while one was open for 0% of the time, Pallas kernels for 0%

commit v1 on v0

v1 whole, which is shorter than its diff:
```python
import functools

import jax
import jax.numpy as jnp
from jax import lax
from jax.experimental import pallas as pl
from jax.experimental.pallas import tpu as pltpu
from jax.sharding import PartitionSpec as P

HEADS = 12
KV_HEADS = 2
HEAD_DIM = 128
PER_KV = HEADS // KV_HEADS
NEG = -1e30
MESH = pl.DeviceIdType.MESH
F32 = jnp.float32
BF16 = jnp.bfloat16


def iota(shape, dim):
    return lax.broadcasted_iota(jnp.int32, shape, dim)


def kernel(
    G, T,
    hid_ref, wq_hbm, wo_hbm, kv_hbm, pt_ref, len_ref, out_ref,
    wq, wo, kv, qsend, qall, qown, bsend, brecv, dsend, drecv, esend, erecv, psend, precv,
    local_sem,
    qs_sem, qr_sem, os_sem, or_sem, bs_sem, br_sem, ds_sem, dr_sem, es_sem, er_sem, ps_sem, pr_sem,
):
    me_g = lax.axis_index("group")
    me_t = lax.axis_index("tp")
    scale = HEAD_DIM ** (-0.5)
    S = kv_hbm.shape[0]
    page_len = kv_hbm.shape[1]
    R = pt_ref.shape[0]
    max_pages = pt_ref.shape[1]
    ring = S * T
    par = lax.rem(me_t, 2)
    hd = HEAD_DIM

    wo_rows = wo_hbm.shape[0]
    wo_base = pl.multiple_of(par * 64, 64)
    cp_wq = pltpu.make_async_copy(wq_hbm, wq, local_sem.at[0])
    cp_kv = pltpu.make_async_copy(kv_hbm, kv, local_sem.at[1])
    cp_wo = pltpu.make_async_copy(wo_hbm, wo.at[pl.ds(wo_base, wo_rows)], local_sem.at[2])
    cp_wq.start()
    cp_kv.start()
    cp_wo.start()

    barrier = pltpu.get_barrier_semaphore()

    def greet_g(d, c):
        pl.semaphore_signal(barrier, inc=1, device_id=(lax.rem(me_g + d, G), me_t), device_id_type=MESH)
        return c

    def greet_t(d, c):
        pl.semaphore_signal(barrier, inc=1, device_id=(me_g, lax.rem(me_t + d, T)), device_id_type=MESH)
        return c

    lax.fori_loop(1, G, greet_g, 0)
    lax.fori_loop(1, T, greet_t, 0)

    zero_base = pl.multiple_of((1 - par) * wo_rows, 64)
    wo[pl.ds(zero_base, 64), :] = jnp.zeros((64, wo.shape[1]), BF16)

    cp_wq.wait()
    qkv = jnp.dot(hid_ref[...], wq[...], preferred_element_type=F32).astype(BF16)
    qsend[...] = qkv
    qall[me_g] = qkv
    qown[me_t] = qkv

    pl.semaphore_wait(barrier, G - 1 + T - 1)

    def to_g(src, dst, ssem, rsem, d, chunked):
        peer = lax.rem(me_g + d, G)
        return pltpu.make_async_remote_copy(
            src_ref=src.at[peer] if chunked else src,
            dst_ref=dst.at[me_g],
            send_sem=ssem.at[d],
            recv_sem=rsem.at[d],
            device_id=(peer, me_t),
            device_id_type=MESH,
        )

    def to_t(src, dst, ssem, rsem, d, chunked):
        peer = lax.rem(me_t + d, T)
        return pltpu.make_async_remote_copy(
            src_ref=src.at[peer] if chunked else src,
            dst_ref=dst.at[me_t],
            send_sem=ssem.at[d],
            recv_sem=rsem.at[d],
            device_id=(me_g, peer),
            device_id_type=MESH,
        )

    def each(n, copy, what):
        def body(d, c):
            getattr(copy(d), what)()
            return c

        lax.fori_loop(1, n, body, 0)

    q_copy = lambda d: to_g(qsend, qall, qs_sem, qr_sem, d, False)
    o_copy = lambda d: to_t(qsend, qown, os_sem, or_sem, d, False)
    b_copy = lambda d: to_t(bsend, brecv, bs_sem, br_sem, d, True)
    d_copy = lambda d: to_t(dsend, drecv, ds_sem, dr_sem, d, True)
    e_copy = lambda d: to_g(esend, erecv, es_sem, er_sem, d, True)
    p_copy = lambda d: to_t(psend, precv, ps_sem, pr_sem, d, True)

    each(G, q_copy, "start")
    each(T, o_copy, "start")

    slot = me_g * ring + iota((R, ring), 1)
    table = pt_ref[...]
    length_row = len_ref[...]
    length_col = jnp.sum(
        jnp.where(iota((R, R), 0) == iota((R, R), 1), jnp.broadcast_to(length_row, (R, R)), 0),
        axis=1, keepdims=True,
    )
    marks = jnp.zeros((R, ring), jnp.int32)
    for j in range(max_pages):
        marks = jnp.where(table[:, j : j + 1] == slot, j + 1, marks)
    owns = marks > 0
    live_row = jnp.sum(
        jnp.where(owns, length_col - (marks - 1) * page_len, 0), axis=0, keepdims=True
    )
    mine = iota((S, ring), 1) == me_t * S + iota((S, ring), 0)
    live_col = jnp.sum(
        jnp.where(mine, jnp.broadcast_to(live_row, (S, ring)), 0), axis=1, keepdims=True
    )
    live8 = iota((S, page_len), 1) < live_col
    live = jnp.concatenate([live8.astype(F32)] * PER_KV, axis=0) > 0.5
    owns_b = owns.astype(F32).astype(BF16)

    each(G, q_copy, "wait_recv")
    q_rows = jnp.concatenate([qall[g] for g in range(G)], axis=0)
    chosen = lax.dot_general(
        owns_b, q_rows, (((0,), (0,)), ((), ())), preferred_element_type=F32
    )
    for t in range(T):
        bsend[t] = chosen[t * S : (t + 1) * S, :].astype(BF16)
    brecv[me_t] = bsend[me_t]
    each(T, b_copy, "start")

    cp_kv.wait()
    each(T, b_copy, "wait_recv")

    rows = PER_KV * S
    row_slot = lax.rem(iota((rows, page_len), 0), S)
    tops, totals, sums = [], [], []
    for g in range(KV_HEADS):
        pieces = []
        for j in range(PER_KV):
            h = g * PER_KV + j
            pieces.append(brecv[h // 2].astype(F32)[:, (h % 2) * hd : (h % 2 + 1) * hd])
        q = jnp.concatenate(pieces, axis=0).astype(BF16)
        scores = jnp.zeros((rows, page_len), F32)
        for s in range(S):
            key = kv[s, :, g * hd : (g + 1) * hd]
            part = lax.dot_general(q, key, (((1,), (1,)), ((), ())), preferred_element_type=F32)
            scores = jnp.where(row_slot == s, part, scores)
        scores = scores * scale
        top = jnp.max(jnp.where(live, scores, NEG), axis=1, keepdims=True)
        prob = jnp.where(live, jnp.exp(scores - top), 0.0).astype(BF16)
        total = jnp.sum(prob.astype(F32), axis=1, keepdims=True)
        acc = jnp.zeros((rows, hd), F32)
        for s in range(S):
            value = kv[s, :, (KV_HEADS + g) * hd : (KV_HEADS + g + 1) * hd]
            part = jnp.dot(prob, value, preferred_element_type=F32)
            acc = jnp.where(row_slot == s, part, acc)
        for j in range(PER_KV):
            cut = slice(j * S, (j + 1) * S)
            tops.append(top[cut])
            totals.append(total[cut])
            sums.append(acc[cut])

    lane8 = iota((S, hd), 1)
    for t in range(T):
        h = (3 * t) // 2
        dsend[t, :, 0:hd] = sums[h]
        dsend[t, :, hd : 2 * hd] = sums[h + 1]
        dsend[t, :, 2 * hd : 3 * hd] = jnp.where(
            lane8 == 0, tops[h],
            jnp.where(lane8 == 1, tops[h + 1], jnp.where(lane8 == 2, totals[h], totals[h + 1])),
        )
    drecv[me_t] = dsend[me_t]
    each(T, d_copy, "start")
    each(T, d_copy, "wait_recv")

    got = drecv[...].reshape(ring, 3 * hd)
    stats = got[:, 2 * hd : 3 * hd]
    same = iota((ring, ring), 0) == iota((ring, ring), 1)
    peaks, wholes, outs = [], [], []
    for i in range(2):
        m_row = jnp.sum(jnp.where(same, stats[:, i : i + 1], 0.0), axis=0, keepdims=True)
        m_all = jnp.where(owns, jnp.broadcast_to(m_row, (R, ring)), NEG)
        peak = jnp.max(m_all, axis=1, keepdims=True)
        weight = jnp.exp(jnp.where(owns, m_row - peak, NEG))
        both = jnp.concatenate([got[:, i * hd : (i + 1) * hd], stats], axis=1)
        mixed = jnp.dot(
            weight, both, preferred_element_type=F32, precision=lax.Precision.HIGHEST
        )
        peaks.append(peak)
        wholes.append(mixed[:, hd + 2 + i : hd + 3 + i])
        outs.append(mixed[:, :hd])
    lane_r = iota((R, hd), 1)
    mixed_stats = jnp.where(
        lane_r == 0, peaks[0],
        jnp.where(lane_r == 1, peaks[1], jnp.where(lane_r == 2, wholes[0], wholes[1])),
    )
    packed = jnp.concatenate([outs[0], outs[1], mixed_stats], axis=1)
    per = R // G
    for g in range(G):
        esend[g] = packed[g * per : (g + 1) * per, :]
    erecv[me_g] = esend[me_g]
    each(G, e_copy, "start")

    each(T, o_copy, "wait_recv")
    first = lax.div(3 * me_t, 2)

    def own_head(h):
        pair = qown[lax.div(h, 2)].astype(F32)
        return jnp.where(lax.rem(h, 2) == 0, pair[:, :hd], pair[:, hd:])

    def own_kv(row, h):
        pair = qown[row].astype(F32)
        return jnp.where(lax.div(h, PER_KV) == 0, pair[:, :hd], pair[:, hd:])

    own_scores = [
        jnp.sum(own_head(first + i) * own_kv(6, first + i), axis=1, keepdims=True) * scale
        for i in range(2)
    ]
    own_values = [own_kv(7, first + i) for i in range(2)]
    cp_wo.wait()
    each(G, e_copy, "wait_recv")

    every = erecv[...]
    heads = []
    for i in range(2):
        m = every[:, :, 2 * hd + i : 2 * hd + i + 1]
        l = every[:, :, 2 * hd + 2 + i : 2 * hd + 3 + i]
        peak = jnp.maximum(jnp.max(m, axis=0), own_scores[i])
        f = jnp.exp(m - peak[None])
        own_f = jnp.exp(own_scores[i] - peak)
        whole = jnp.sum(f * l, axis=0) + own_f
        summed = jnp.sum(f * every[:, :, i * hd : (i + 1) * hd], axis=0) + own_f * own_values[i]
        heads.append(summed / whole)
    attn = jnp.concatenate(heads, axis=1)
    col = iota(attn.shape, 1)
    attn = jnp.where((col >= par * 64) & (col < par * 64 + wo_rows), attn, 0.0).astype(BF16)
    part = jnp.dot(attn, wo[...], preferred_element_type=F32)
    width = out_ref.shape[1]
    for t in range(T):
        psend[t] = part[:, t * width : (t + 1) * width]
    precv[me_t] = psend[me_t]
    each(T, p_copy, "start")
    each(T, p_copy, "wait_recv")
    out_ref[...] = jnp.sum(precv[...], axis=0).astype(BF16)

    each(G, q_copy, "wait_send")
    each(T, o_copy, "wait_send")
    each(T, b_copy, "wait_send")
    each(T, d_copy, "wait_send")
    each(G, e_copy, "wait_send")
    each(T, p_copy, "wait_send")


def solution(mesh):
    G, T = mesh.shape["group"], mesh.shape["tp"]

    def on_device(hidden_in, w_qkv, w_out, kv_pool, page_table, lengths):
        per = hidden_in.shape[0]
        cols = w_qkv.shape[1]
        slots = kv_pool.shape[0]
        depth = w_out.shape[1]
        width = depth // T
        wide = 3 * HEAD_DIM
        dma = pltpu.SemaphoreType.DMA
        vm = pl.BlockSpec(memory_space=pltpu.VMEM)
        hbm = pl.BlockSpec(memory_space=pl.ANY)
        return pl.pallas_call(
            functools.partial(kernel, G, T),
            name="decode",
            out_shape=jax.ShapeDtypeStruct((per, width), BF16),
            in_specs=[vm, hbm, hbm, hbm, vm, vm],
            out_specs=vm,
            scratch_shapes=[
                pltpu.VMEM(w_qkv.shape, BF16),
                pltpu.VMEM((2 * HEAD_DIM, depth), BF16),
                pltpu.VMEM(kv_pool.shape, BF16),
                pltpu.VMEM((per, cols), BF16),
                pltpu.VMEM((G, per, cols), BF16),
                pltpu.VMEM((T, per, cols), BF16),
                pltpu.VMEM((T, slots, cols), BF16),
                pltpu.VMEM((T, slots, cols), BF16),
                pltpu.VMEM((T, slots, wide), F32),
                pltpu.VMEM((T, slots, wide), F32),
                pltpu.VMEM((G, per, wide), F32),
                pltpu.VMEM((G, per, wide), F32),
                pltpu.VMEM((T, per, width), F32),
                pltpu.VMEM((T, per, width), F32),
                dma((3,)),
                dma((G,)), dma((G,)), dma((T,)), dma((T,)), dma((T,)), dma((T,)),
                dma((T,)), dma((T,)), dma((G,)), dma((G,)), dma((T,)), dma((T,)),
            ],
            compiler_params=pltpu.CompilerParams(collective_id=0, has_side_effects=True),
        )(hidden_in, w_qkv, w_out, kv_pool, page_table, lengths.reshape(1, -1))

    return jax.shard_map(
        on_device,
        mesh=mesh,
        in_specs=(
            P("group", None),
            P(None, "tp"),
            P("tp", None),
            P(("group", "tp"), None, None),
            P(),
            P(),
        ),
        out_specs=P("group", "tp"),
        check_vma=False,
    )
```

time: 430 us -> 43.2 us (0.10)
  waiting for transfers between devices: 204 us -> 0 us
  blocking collectives: 194 us -> 0 us
  Pallas kernels: 0 us -> 40.4 us
  between operations: 13.6 us -> 0.01 us
  matrix products: 5.2 us -> 0 us
    psum x1 -> x0, waiting for transfers between devices: 169 us -> none  [on_device(): lax.psum((req_total * rescale, req_sums * jnp.repeat(rescale, HEAD_DIM, a...]
    psum x1 -> x0, blocking collectives: 74.9 us -> none  [on_device(): lax.psum((req_total * rescale, req_sums * jnp.repeat(rescale, HEAD_DIM, a...]
    pmax x1 -> x0, blocking collectives: 73.4 us -> none  [on_device(): peak_all = lax.pmax(req_top, ('group', 'tp'))]
    all_gather x2 -> x0, blocking collectives: 45.5 us -> none  [the longest x1 29 us: on_device(): queries = lax.all_gather(qkv[:, :qdim], 'group', axis=0, tiled=True)]
    pallas_call x0 -> x1, Pallas kernels: none -> 40.4 us  [on_device(): pl.pallas_call(functools.partial(kernel, G, T), name='decode', out_shape=...]
    unnamed x3 -> x0, waiting for transfers between devices: 35.3 us -> none
  transfers between devices with their start and end apart: 2 -> 0, of which waited for: 2 -> 0; matrix products, arithmetic and copies ran while one was open for 0% -> 0% of each run, Pallas kernels for 0% -> 0%
where the time goes in v1:
time: 43.2 us; the launch traced here: 43 us
  Pallas kernels  40.4 us (94%)
  local copies, waits for them, and re-layouts  2.62 us (6%)
    pallas_call x1, Pallas kernels, on_device(): pl.pallas_call(functools.partial(kernel, G, T), name='decode', out_shape=...  40.4 us
    unnamed x2, local copies, waits for them, and re-layouts  2.62 us

profile of v1, /device:TPU:1, one launch (start us, length us, event | category | flops | bytes accessed | tf_op | source)
XLA Modules:
  0.0 43.0 jit_solution(498662748465572536)
XLA Ops:
  0.0 1.4 %copy.7.pt_ref = s32[64,32]{1,0:T(8,128)} copy(s32[64,32]{0,1:T(8,128)} %param.10) | data formatting | bytes 16384 | tf_op args[4]
  1.4 40.4 %decode.1 = bf16[2,384]{1,0:T(2,128)(2,1)} custom-call(bf16[2,3072]{1,0:T(2,128)(2,1)} %hid_ref.1, bf16[3072,256]{1,0:T(8,128)(2,1)} %wq_hbm.1, bf16[192,3072]{1,0:T(8,128)(2,1)} %wo_hbm.1, bf16[8,128,512]{2,1,0:T(8,128)(2,1)} %kv_hbm.1, s32[64,32]{1,0:T(8,128)} %copy.7.pt_ref, s32[1,64]{1,0:T(1,128)} %bitcast.1), custom_call_target="tpu_custom_call" | custom-call | tf_op jit(solution)/shard_map/decode/pallas_call | solution.py:282
  41.8 1.2 %copy.9 = bf16[2,384]{1,0:T(2,128)(2,1)} copy(bf16[2,384]{1,0:T(2,128)(2,1)} %decode.1) | data formatting | bytes 3072

commit v2 on v1

v2 whole, which is shorter than its diff:
```python
import functools

import jax
import jax.numpy as jnp
from jax import lax
from jax.experimental import pallas as pl
from jax.experimental.pallas import tpu as pltpu
from jax.sharding import PartitionSpec as P

HEADS = 12
KV_HEADS = 2
HEAD_DIM = 128
PER_KV = HEADS // KV_HEADS
NEG = -1e30
MESH = pl.DeviceIdType.MESH
F32 = jnp.float32
BF16 = jnp.bfloat16


def iota(shape, dim):
    return lax.broadcasted_iota(jnp.int32, shape, dim)


def pieces3(x):
    hi = x.astype(BF16).astype(F32)
    mid = (x - hi).astype(BF16).astype(F32)
    return [hi, mid, x - hi - mid]


def order_t(T):
    return sorted(range(1, T), key=lambda d: -min(d, T - d))


def order_g(n):
    hops = lambda d: min(d, n - d)
    all_d = [(x, y, c) for x in range(n) for y in range(n) for c in range(2)]
    return sorted(all_d[1:], key=lambda o: -(hops(o[0]) + hops(o[1])) * 2 - o[2])


def spread(columns, lane, width):
    out = columns[-1]
    for i in range(len(columns) - 2, -1, -1):
        out = jnp.where(lane == i, columns[i], out)
    return jnp.broadcast_to(out, (out.shape[0], width))


def kernel(
    G, T,
    hid_hbm, wq_hbm, wo_hbm, kv_hbm, pt_hbm, len_hbm, out_ref,
    hid, pt, lens, wq, wo, kv,
    qsend, qall, qown, bsend, brecv, dsend, drecv, esend, erecv, psend, precv,
    local_sem, send_sem, recv_sem,
):
    me_g = lax.axis_index("group")
    me_t = lax.axis_index("tp")
    scale = HEAD_DIM ** (-0.5)
    S = kv_hbm.shape[0]
    page_len = kv_hbm.shape[1]
    max_pages, R = pt_hbm.shape
    ring = S * T
    par = lax.rem(me_t, 2)
    hd = HEAD_DIM
    side = 1
    while 2 * side * side < G:
        side += 1

    xs = [lax.rem(lax.div(me_g, 2 * side) + d, side) * (2 * side) for d in range(side)]
    ys = [lax.rem(lax.rem(lax.div(me_g, 2), side) + d, side) * 2 for d in range(side)]
    cs = [lax.rem(lax.rem(me_g, 2) + d, 2) for d in range(2)]
    peers_g = [xs[dx] + ys[dy] + cs[dc] for dx, dy, dc in order_g(side)]
    peers_t = [lax.rem(me_t + d, T) for d in order_t(T)]

    barrier = pltpu.get_barrier_semaphore()
    for p in peers_t:
        pl.semaphore_signal(barrier, inc=1, device_id=(me_g, p), device_id_type=MESH)
    for p in peers_g:
        pl.semaphore_signal(barrier, inc=1, device_id=(p, me_t), device_id_type=MESH)

    wo_rows = wo_hbm.shape[0]
    wo_base = pl.multiple_of(par * 64, 64)
    loads = [
        pltpu.make_async_copy(src, dst, local_sem.at[i])
        for i, (src, dst) in enumerate([
            (hid_hbm, hid), (wq_hbm, wq), (pt_hbm, pt), (len_hbm, lens), (kv_hbm, kv),
            (wo_hbm, wo.at[pl.ds(wo_base, wo_rows)]),
        ])
    ]
    for load in loads:
        load.start()
    cp_hid, cp_wq, cp_pt, cp_len, cp_kv, cp_wo = loads

    zero_base = pl.multiple_of((1 - par) * wo_rows, 64)
    wo[pl.ds(zero_base, 64), :] = jnp.zeros((64, wo.shape[1]), BF16)

    cp_hid.wait()
    cp_wq.wait()
    qkv = jnp.dot(hid[...], wq[...], preferred_element_type=F32).astype(BF16)
    qsend[...] = qkv
    qall[me_g] = qkv
    qown[me_t] = qkv

    def send_g(k, src, dst, chunked):
        for p in peers_g:
            pltpu.make_async_remote_copy(
                src_ref=src.at[p] if chunked else src, dst_ref=dst.at[me_g],
                send_sem=send_sem.at[k], recv_sem=recv_sem.at[k],
                device_id=(p, me_t), device_id_type=MESH,
            ).start()

    def send_t(k, src, dst, chunked):
        for p in peers_t:
            pltpu.make_async_remote_copy(
                src_ref=src.at[p] if chunked else src, dst_ref=dst.at[me_t],
                send_sem=send_sem.at[k], recv_sem=recv_sem.at[k],
                device_id=(me_g, p), device_id_type=MESH,
            ).start()

    def wait(sems, k, dst):
        most = dst.at[pl.ds(0, dst.shape[0] - 1)]
        pltpu.make_async_copy(most, most, sems.at[k]).wait()

    pl.semaphore_wait(barrier, G - 1 + T - 1)
    send_g(0, qsend, qall, False)
    send_t(1, qsend, qown, False)

    cp_pt.wait()
    cp_len.wait()

    def find(first, count):
        slot = first + iota((count, R), 0)
        marks = jnp.zeros((count, R), jnp.int32)
        for j in range(max_pages):
            marks = jnp.where(pt[j : j + 1, :] == slot, j + 1, marks)
        return marks

    held = (find(me_g * ring, ring) > 0).astype(F32).astype(BF16)
    eye = (iota((R, R), 0) == iota((R, R), 1)).astype(F32).astype(BF16)
    owns = lax.dot_general(
        eye, held, (((1,), (1,)), ((), ())), preferred_element_type=F32
    ) > 0.5
    marks = find(me_g * ring + me_t * S, S)
    live_col = jnp.sum(
        jnp.where(marks > 0, lens[...] - (marks - 1) * page_len, 0), axis=1, keepdims=True
    )
    live8 = iota((S, page_len), 1) < live_col
    live = jnp.concatenate([live8.astype(F32)] * PER_KV, axis=0) > 0.5

    wait(recv_sem, 0, qall)
    q_rows = jnp.concatenate([qall[g] for g in range(G)], axis=0)
    chosen = jnp.dot(held, q_rows, preferred_element_type=F32)
    for t in range(T):
        bsend[t] = chosen[t * S : (t + 1) * S, :].astype(BF16)
    brecv[me_t] = bsend[me_t]
    send_t(2, bsend, brecv, True)

    cp_kv.wait()
    wait(recv_sem, 2, brecv)

    rows = PER_KV * S
    row_slot = lax.rem(iota((rows, page_len), 0), S)
    tops, totals, sums = [], [], []
    for g in range(KV_HEADS):
        parts = []
        for j in range(PER_KV):
            h = g * PER_KV + j
            parts.append(brecv[h // 2].astype(F32)[:, (h % 2) * hd : (h % 2 + 1) * hd])
        q = jnp.concatenate(parts, axis=0).astype(BF16)
        scores = jnp.zeros((rows, page_len), F32)
        for s in range(S):
            key = kv[s, :, g * hd : (g + 1) * hd]
            part = lax.dot_general(q, key, (((1,), (1,)), ((), ())), preferred_element_type=F32)
            scores = jnp.where(row_slot == s, part, scores)
        scores = scores * scale
        top = jnp.max(jnp.where(live, scores, NEG), axis=1, keepdims=True)
        prob = jnp.where(live, jnp.exp(scores - top), 0.0).astype(BF16)
        total = jnp.sum(prob.astype(F32), axis=1, keepdims=True)
        acc = jnp.zeros((rows, hd), F32)
        for s in range(S):
            value = kv[s, :, (KV_HEADS + g) * hd : (KV_HEADS + g + 1) * hd]
            part = jnp.dot(prob, value, preferred_element_type=F32)
            acc = jnp.where(row_slot == s, part, acc)
        for j in range(PER_KV):
            cut = slice(j * S, (j + 1) * S)
            tops.append(pieces3(top[cut]))
            totals.append(pieces3(total[cut]))
            sums.append(acc[cut])

    lane8 = iota((S, hd), 1)
    for t in range(T):
        h = (3 * t) // 2
        stats = spread(tops[h] + tops[h + 1] + totals[h] + totals[h + 1], lane8, hd)
        dsend[t] = jnp.concatenate([sums[h], sums[h + 1], stats], axis=1).astype(BF16)
    drecv[me_t] = dsend[me_t]
    send_t(3, dsend, drecv, True)
    wait(recv_sem, 3, drecv)

    got = drecv[...].astype(F32).reshape(ring, 3 * hd)
    same = iota((ring, ring), 0) == iota((ring, ring), 1)
    peaks, weights = [], []
    for i in range(2):
        c = 2 * hd + 3 * i
        m_col = got[:, c : c + 1] + got[:, c + 1 : c + 2] + got[:, c + 2 : c + 3]
        m_row = jnp.sum(jnp.where(same, m_col, 0.0), axis=0, keepdims=True)
        peak = jnp.max(jnp.where(owns, m_row, NEG), axis=1, keepdims=True)
        weight = jnp.exp(jnp.where(owns, m_row - peak, NEG))
        peaks.append(peak)
        high = weight.astype(BF16).astype(F32)
        weights += [high, weight - high]
    mixed = jnp.dot(
        jnp.concatenate(weights, axis=0).astype(BF16), got.astype(BF16),
        preferred_element_type=F32,
    )
    wholes, outs = [], []
    for i in range(2):
        both = mixed[2 * i * R : (2 * i + 1) * R] + mixed[(2 * i + 1) * R : (2 * i + 2) * R]
        c = 2 * hd + 6 + 3 * i
        wholes.append(both[:, c : c + 1] + both[:, c + 1 : c + 2] + both[:, c + 2 : c + 3])
        outs.append(both[:, i * hd : (i + 1) * hd])
    mixed_stats = spread(peaks + wholes, iota((R, hd), 1), hd)
    packed = jnp.concatenate(outs + [mixed_stats], axis=1)
    per = R // G
    for g in range(G):
        esend[g] = packed[g * per : (g + 1) * per, :]
    erecv[me_g] = esend[me_g]
    send_g(4, esend, erecv, True)

    wait(recv_sem, 1, qown)
    first = lax.div(3 * me_t, 2)

    def own_head(h):
        pair = qown[lax.div(h, 2)].astype(F32)
        return jnp.where(lax.rem(h, 2) == 0, pair[:, :hd], pair[:, hd:])

    def own_kv(row, h):
        pair = qown[row].astype(F32)
        return jnp.where(lax.div(h, PER_KV) == 0, pair[:, :hd], pair[:, hd:])

    own_scores = [
        jnp.sum(own_head(first + i) * own_kv(6, first + i), axis=1, keepdims=True) * scale
        for i in range(2)
    ]
    own_values = [own_kv(7, first + i) for i in range(2)]
    cp_wo.wait()
    wait(recv_sem, 4, erecv)

    every = erecv[...]
    heads = []
    for i in range(2):
        m = every[:, :, 2 * hd + i : 2 * hd + i + 1]
        l = every[:, :, 2 * hd + 2 + i : 2 * hd + 3 + i]
        peak = jnp.maximum(jnp.max(m, axis=0), own_scores[i])
        f = jnp.exp(m - peak[None])
        own_f = jnp.exp(own_scores[i] - peak)
        whole = jnp.sum(f * l, axis=0) + own_f
        summed = jnp.sum(f * every[:, :, i * hd : (i + 1) * hd], axis=0) + own_f * own_values[i]
        heads.append(summed / whole)
    attn = jnp.concatenate(heads, axis=1)
    col = iota(attn.shape, 1)
    attn = jnp.where((col >= par * 64) & (col < par * 64 + wo_rows), attn, 0.0).astype(BF16)
    part = jnp.dot(attn, wo[...], preferred_element_type=F32)
    width = out_ref.shape[1]
    for t in range(T):
        psend[t] = part[:, t * width : (t + 1) * width]
    precv[me_t] = psend[me_t]
    send_t(5, psend, precv, True)
    wait(recv_sem, 5, precv)
    out_ref[...] = jnp.sum(precv[...], axis=0).astype(BF16)

    for k, dst in enumerate([qall, qown, brecv, drecv, erecv, precv]):
        wait(send_sem, k, dst)


def solution(mesh):
    G, T = mesh.shape["group"], mesh.shape["tp"]

    def on_device(hidden_in, w_qkv, w_out, kv_pool, page_table, lengths):
        per = hidden_in.shape[0]
        cols = w_qkv.shape[1]
        slots = kv_pool.shape[0]
        depth = w_out.shape[1]
        width = depth // T
        wide = 3 * HEAD_DIM
        dma = pltpu.SemaphoreType.DMA
        vm = pl.BlockSpec(memory_space=pltpu.VMEM)
        hbm = pl.BlockSpec(memory_space=pl.ANY)
        return pl.pallas_call(
            functools.partial(kernel, G, T),
            name="decode",
            out_shape=jax.ShapeDtypeStruct((per, width), BF16),
            in_specs=[hbm] * 6,
            out_specs=vm,
            scratch_shapes=[
                pltpu.VMEM(hidden_in.shape, BF16),
                pltpu.VMEM(page_table.shape[::-1], jnp.int32),
                pltpu.VMEM((1, lengths.shape[0]), jnp.int32),
                pltpu.VMEM(w_qkv.shape, BF16),
                pltpu.VMEM((2 * HEAD_DIM, depth), BF16),
                pltpu.VMEM(kv_pool.shape, BF16),
                pltpu.VMEM((per, cols), BF16),
                pltpu.VMEM((G, per, cols), BF16),
                pltpu.VMEM((T, per, cols), BF16),
                pltpu.VMEM((T, slots, cols), BF16),
                pltpu.VMEM((T, slots, cols), BF16),
                pltpu.VMEM((T, slots, wide), BF16),
                pltpu.VMEM((T, slots, wide), BF16),
                pltpu.VMEM((G, per, wide), F32),
                pltpu.VMEM((G, per, wide), F32),
                pltpu.VMEM((T, per, width), F32),
                pltpu.VMEM((T, per, width), F32),
                dma((6,)), dma((6,)), dma((6,)),
            ],
            compiler_params=pltpu.CompilerParams(collective_id=0, has_side_effects=True),
        )(hidden_in, w_qkv, w_out, kv_pool, page_table.T, lengths.reshape(1, -1))

    return jax.shard_map(
        on_device,
        mesh=mesh,
        in_specs=(
            P("group", None),
            P(None, "tp"),
            P("tp", None),
            P(("group", "tp"), None, None),
            P(),
            P(),
        ),
        out_specs=P("group", "tp"),
        check_vma=False,
    )
```

time: 43.2 us -> 37.4 us (0.87)
  Pallas kernels: 40.4 us -> 36 us
  local copies, waits for them, and re-layouts: 2.62 us -> 1.25 us
    pallas_call x1, Pallas kernels: 40.4 us -> 36 us  [on_device(): pl.pallas_call(functools.partial(kernel, G, T), name='decode', out_shape=...]
    unnamed x2 -> x1, local copies, waits for them, and re-layouts: 2.62 us -> 1.25 us
where the time goes in v2:
time: 37.4 us; the launch traced here: 37.3 us
  Pallas kernels  36 us (96%)
  local copies, waits for them, and re-layouts  1.25 us (3%)
    pallas_call x1, Pallas kernels, on_device(): pl.pallas_call(functools.partial(kernel, G, T), name='decode', out_shape=...  36 us
    unnamed x1, local copies, waits for them, and re-layouts  1.25 us

profile of v2, /device:TPU:1, one launch (start us, length us, event | category | flops | bytes accessed | tf_op | source)
XLA Modules:
  0.0 37.3 jit_solution(4092127334829875308)
XLA Ops:
  0.0 36.0 %decode.1 = bf16[2,384]{1,0:T(2,128)(2,1)} custom-call(bf16[2,3072]{1,0:T(2,128)(2,1)} %hid_hbm.1, bf16[3072,256]{1,0:T(8,128)(2,1)} %wq_hbm.1, bf16[192,3072]{1,0:T(8,128)(2,1)} %wo_hbm.1, bf16[8,128,512]{2,1,0:T(8,128)(2,1)} %kv_hbm.1, s32[32,64]{1,0:T(8,128)} %bitcast.2, s32[1,64]{1,0:T(1,128)} %bitcast.3), custom_call_target="tpu_custom_call" | custom-call | tf_op jit(solution)/shard_map/decode/pallas_call | solution.py:286
  36.0 1.2 %copy.8 = bf16[2,384]{1,0:T(2,128)(2,1)} copy(bf16[2,384]{1,0:T(2,128)(2,1)} %decode.1) | data formatting | bytes 3072

commit v3 on v2

--- a/solution.py
+++ b/solution.py
@@ -21,12 +21,6 @@
     return lax.broadcasted_iota(jnp.int32, shape, dim)
 
 
-def pieces3(x):
-    hi = x.astype(BF16).astype(F32)
-    mid = (x - hi).astype(BF16).astype(F32)
-    return [hi, mid, x - hi - mid]
-
-
 def order_t(T):
     return sorted(range(1, T), key=lambda d: -min(d, T - d))
 
@@ -46,9 +40,9 @@
 
 def kernel(
     G, T,
-    hid_hbm, wq_hbm, wo_hbm, kv_hbm, pt_hbm, len_hbm, out_ref,
+    hid_hbm, wq_hbm, wo_hbm, kv_hbm, pt_hbm, len_hbm, precv,
     hid, pt, lens, wq, wo, kv,
-    qsend, qall, qown, bsend, brecv, dsend, drecv, esend, erecv, psend, precv,
+    qsend, qall, qown, bsend, brecv, dsend, drecv, esend, erecv, psend,
     local_sem, send_sem, recv_sem,
 ):
     me_g = lax.axis_index("group")
@@ -143,7 +137,7 @@
         jnp.where(marks > 0, lens[...] - (marks - 1) * page_len, 0), axis=1, keepdims=True
     )
     live8 = iota((S, page_len), 1) < live_col
-    live = jnp.concatenate([live8.astype(F32)] * PER_KV, axis=0) > 0.5
+    live = jnp.concatenate([live8.astype(F32)] * HEADS, axis=0) > 0.5
 
     wait(recv_sem, 0, qall)
     q_rows = jnp.concatenate([qall[g] for g in range(G)], axis=0)
@@ -156,40 +150,48 @@
     cp_kv.wait()
     wait(recv_sem, 2, brecv)
 
-    rows = PER_KV * S
+    rows = HEADS * S
+    kdim = KV_HEADS * hd
     row_slot = lax.rem(iota((rows, page_len), 0), S)
-    tops, totals, sums = [], [], []
-    for g in range(KV_HEADS):
-        parts = []
-        for j in range(PER_KV):
-            h = g * PER_KV + j
-            parts.append(brecv[h // 2].astype(F32)[:, (h % 2) * hd : (h % 2 + 1) * hd])
-        q = jnp.concatenate(parts, axis=0).astype(BF16)
-        scores = jnp.zeros((rows, page_len), F32)
-        for s in range(S):
-            key = kv[s, :, g * hd : (g + 1) * hd]
-            part = lax.dot_general(q, key, (((1,), (1,)), ((), ())), preferred_element_type=F32)
-            scores = jnp.where(row_slot == s, part, scores)
-        scores = scores * scale
-        top = jnp.max(jnp.where(live, scores, NEG), axis=1, keepdims=True)
-        prob = jnp.where(live, jnp.exp(scores - top), 0.0).astype(BF16)
-        total = jnp.sum(prob.astype(F32), axis=1, keepdims=True)
-        acc = jnp.zeros((rows, hd), F32)
-        for s in range(S):
-            value = kv[s, :, (KV_HEADS + g) * hd : (KV_HEADS + g + 1) * hd]
-            part = jnp.dot(prob, value, preferred_element_type=F32)
-            acc = jnp.where(row_slot == s, part, acc)
-        for j in range(PER_KV):
-            cut = slice(j * S, (j + 1) * S)
-            tops.append(pieces3(top[cut]))
-            totals.append(pieces3(total[cut]))
-            sums.append(acc[cut])
-
+    empty = jnp.zeros((S, hd), F32)
+    lines = []
+    for h in range(HEADS):
+        line = brecv[h // 2].astype(F32)[:, (h % 2) * hd : (h % 2 + 1) * hd]
+        lines.append([line if g == h // PER_KV else empty for g in range(KV_HEADS)])
+    q = jnp.concatenate(
+        [jnp.concatenate([line[g] for line in lines], axis=0) for g in range(KV_HEADS)], axis=1
+    ).astype(BF16)
+    scores = jnp.zeros((rows, page_len), F32)
+    for s in range(0, S, 2):
+        key = kv[s : s + 2, :, 0:kdim].reshape(2 * page_len, kdim)
+        part = lax.dot_general(q, key, (((1,), (1,)), ((), ())), preferred_element_type=F32)
+        scores = jnp.where(row_slot == s, part[:, :page_len], scores)
+        scores = jnp.where(row_slot == s + 1, part[:, page_len:], scores)
+    scores = scores * scale
+    top = jnp.max(jnp.where(live, scores, NEG), axis=1, keepdims=True)
+    prob = jnp.where(live, jnp.exp(scores - top), 0.0).astype(BF16).astype(F32)
+    total = jnp.sum(prob, axis=1, keepdims=True)
+    acc = jnp.zeros((rows, kdim), F32)
+    for s in range(0, S, 2):
+        value = kv[s : s + 2, :, kdim : 2 * kdim].reshape(2 * page_len, kdim)
+        pair = jnp.concatenate([jnp.where(row_slot == s + k, prob, 0.0) for k in range(2)], axis=1)
+        acc = acc + jnp.dot(pair.astype(BF16), value, preferred_element_type=F32)
+
+    lane = lax.rem(iota((rows, hd), 1), hd // 2)
+    both = jnp.where(lane < 3, top, total)
+    high = both.astype(BF16).astype(F32)
+    mid = (both - high).astype(BF16).astype(F32)
+    kind = lax.rem(lane, 3)
+    stats = jnp.where(kind == 0, high, jnp.where(kind == 1, mid, both - high - mid))
     lane8 = iota((S, hd), 1)
+    cut = lambda h: slice(h * S, (h + 1) * S)
+    head_sum = lambda h: acc[cut(h), (h // PER_KV) * hd : (h // PER_KV + 1) * hd]
     for t in range(T):
         h = (3 * t) // 2
-        stats = spread(tops[h] + tops[h + 1] + totals[h] + totals[h + 1], lane8, hd)
-        dsend[t] = jnp.concatenate([sums[h], sums[h + 1], stats], axis=1).astype(BF16)
+        pair_stats = jnp.where(lane8 < hd // 2, stats[cut(h)], stats[cut(h + 1)])
+        dsend[t] = jnp.concatenate(
+            [head_sum(h), head_sum(h + 1), pair_stats], axis=1
+        ).astype(BF16)
     drecv[me_t] = dsend[me_t]
     send_t(3, dsend, drecv, True)
     wait(recv_sem, 3, drecv)
@@ -198,7 +200,7 @@
     same = iota((ring, ring), 0) == iota((ring, ring), 1)
     peaks, weights = [], []
     for i in range(2):
-        c = 2 * hd + 3 * i
+        c = 2 * hd + (hd // 2) * i
         m_col = got[:, c : c + 1] + got[:, c + 1 : c + 2] + got[:, c + 2 : c + 3]
         m_row = jnp.sum(jnp.where(same, m_col, 0.0), axis=0, keepdims=True)
         peak = jnp.max(jnp.where(owns, m_row, NEG), axis=1, keepdims=True)
@@ -213,7 +215,7 @@
     wholes, outs = [], []
     for i in range(2):
         both = mixed[2 * i * R : (2 * i + 1) * R] + mixed[(2 * i + 1) * R : (2 * i + 2) * R]
-        c = 2 * hd + 6 + 3 * i
+        c = 2 * hd + (hd // 2) * i + 3
         wholes.append(both[:, c : c + 1] + both[:, c + 1 : c + 2] + both[:, c + 2 : c + 3])
         outs.append(both[:, i * hd : (i + 1) * hd])
     mixed_stats = spread(peaks + wholes, iota((R, hd), 1), hd)
@@ -258,13 +260,14 @@
     col = iota(attn.shape, 1)
     attn = jnp.where((col >= par * 64) & (col < par * 64 + wo_rows), attn, 0.0).astype(BF16)
     part = jnp.dot(attn, wo[...], preferred_element_type=F32)
-    width = out_ref.shape[1]
+    width = precv.shape[2]
     for t in range(T):
         psend[t] = part[:, t * width : (t + 1) * width]
-    precv[me_t] = psend[me_t]
     send_t(5, psend, precv, True)
+    cp_own = pltpu.make_async_copy(psend.at[me_t], precv.at[me_t], local_sem.at[6])
+    cp_own.start()
     wait(recv_sem, 5, precv)
-    out_ref[...] = jnp.sum(precv[...], axis=0).astype(BF16)
+    cp_own.wait()
 
     for k, dst in enumerate([qall, qown, brecv, drecv, erecv, precv]):
         wait(send_sem, k, dst)
@@ -283,12 +286,12 @@
         dma = pltpu.SemaphoreType.DMA
         vm = pl.BlockSpec(memory_space=pltpu.VMEM)
         hbm = pl.BlockSpec(memory_space=pl.ANY)
-        return pl.pallas_call(
+        parts = pl.pallas_call(
             functools.partial(kernel, G, T),
             name="decode",
-            out_shape=jax.ShapeDtypeStruct((per, width), BF16),
+            out_shape=jax.ShapeDtypeStruct((T, per, width), F32),
             in_specs=[hbm] * 6,
-            out_specs=vm,
+            out_specs=hbm,
             scratch_shapes=[
                 pltpu.VMEM(hidden_in.shape, BF16),
                 pltpu.VMEM(page_table.shape[::-1], jnp.int32),
@@ -306,11 +309,11 @@
                 pltpu.VMEM((G, per, wide), F32),
                 pltpu.VMEM((G, per, wide), F32),
                 pltpu.VMEM((T, per, width), F32),
-                pltpu.VMEM((T, per, width), F32),
-                dma((6,)), dma((6,)), dma((6,)),
+                dma((7,)), dma((6,)), dma((6,)),
             ],
             compiler_params=pltpu.CompilerParams(collective_id=0, has_side_effects=True),
         )(hidden_in, w_qkv, w_out, kv_pool, page_table.T, lengths.reshape(1, -1))
+        return jnp.sum(parts, axis=0).astype(BF16)
 
     return jax.shard_map(
         on_device,

time: 37.4 us -> 36.5 us (0.976)
  other arithmetic: 0 us -> 1.32 us
  local copies, waits for them, and re-layouts: 1.25 us -> 0 us
  Pallas kernels: 36 us -> 35.1 us
    reduce_sum x0 -> x1, other arithmetic: none -> 1.32 us  [on_device(): return jnp.sum(parts, axis=0).astype(BF16)]
    unnamed x1 -> x0, local copies, waits for them, and re-layouts: 1.25 us -> none
    pallas_call x1, Pallas kernels: 36 us -> 35.1 us  [on_device(): pl.pallas_call(functools.partial(kernel, G, T), name='decode', out_shape=...]
where the time goes in v3:
time: 36.5 us; the launch traced here: 36.4 us
  Pallas kernels  35.1 us (96%)
  other arithmetic  1.32 us (4%)
    pallas_call x1, Pallas kernels, on_device(): pl.pallas_call(functools.partial(kernel, G, T), name='decode', out_shape=...  35.1 us
    reduce_sum x1, other arithmetic, on_device(): return jnp.sum(parts, axis=0).astype(BF16)  1.32 us

profile of v3, /device:TPU:1, one launch (start us, length us, event | category | flops | bytes accessed | tf_op | source)
XLA Modules:
  0.0 36.4 jit_solution(9336430175523885370)
XLA Ops:
  0.0 35.1 %decode.1 = f32[8,2,384]{2,1,0:T(2,128)} custom-call(bf16[2,3072]{1,0:T(2,128)(2,1)} %hid_hbm.1, bf16[3072,256]{1,0:T(8,128)(2,1)} %wq_hbm.1, bf16[192,3072]{1,0:T(8,128)(2,1)} %wo_hbm.1, bf16[8,128,512]{2,1,0:T(8,128)(2,1)} %kv_hbm.1, s32[32,64]{1,0:T(8,128)} %bitcast.2, s32[1,64]{1,0:T(1,128)} %bitcast.3), custom_call_target="tpu_custom_call" | custom-call | tf_op jit(solution)/shard_map/decode/pallas_call | solution.py:289
  35.1 1.3 %reduce_sum.9 = bf16[2,384]{1,0:T(2,128)(2,1)} reduce(f32[8,2,384]{2,1,0:T(2,128)} %decode.1, f32[]{:T(128)} %constant.0.clone.1), dimensions={0}, to_apply=%region_0.0 | reduce | flops 5376 | bytes 26116 | tf_op jit(solution)/shard_map/reduce_sum | solution.py:316

commit v4 on v3

--- a/solution.py
+++ b/solution.py
@@ -101,13 +101,16 @@
                 device_id=(p, me_t), device_id_type=MESH,
             ).start()
 
+    def copy_t(k, src, dst, p):
+        return pltpu.make_async_remote_copy(
+            src_ref=src, dst_ref=dst.at[me_t],
+            send_sem=send_sem.at[k], recv_sem=recv_sem.at[k],
+            device_id=(me_g, p), device_id_type=MESH,
+        )
+
     def send_t(k, src, dst, chunked):
         for p in peers_t:
-            pltpu.make_async_remote_copy(
-                src_ref=src.at[p] if chunked else src, dst_ref=dst.at[me_t],
-                send_sem=send_sem.at[k], recv_sem=recv_sem.at[k],
-                device_id=(me_g, p), device_id_type=MESH,
-            ).start()
+            copy_t(k, src.at[p] if chunked else src, dst, p).start()
 
     def wait(sems, k, dst):
         most = dst.at[pl.ds(0, dst.shape[0] - 1)]
@@ -130,7 +133,8 @@
     held = (find(me_g * ring, ring) > 0).astype(F32).astype(BF16)
     eye = (iota((R, R), 0) == iota((R, R), 1)).astype(F32).astype(BF16)
     owns = lax.dot_general(
-        eye, held, (((1,), (1,)), ((), ())), preferred_element_type=F32
+        eye, jnp.concatenate([held, held], axis=0), (((1,), (1,)), ((), ())),
+        preferred_element_type=F32,
     ) > 0.5
     marks = find(me_g * ring + me_t * S, S)
     live_col = jnp.sum(
@@ -197,27 +201,26 @@
     wait(recv_sem, 3, drecv)
 
     got = drecv[...].astype(F32).reshape(ring, 3 * hd)
-    same = iota((ring, ring), 0) == iota((ring, ring), 1)
-    peaks, weights = [], []
+    stats = got[:, 2 * hd : 3 * hd]
+    half = iota((R, 2 * ring), 1) < ring
+    same = iota((ring, 2 * ring), 0) == lax.rem(iota((ring, 2 * ring), 1), ring)
+    peaks, wholes, outs = [], [], []
     for i in range(2):
-        c = 2 * hd + (hd // 2) * i
-        m_col = got[:, c : c + 1] + got[:, c + 1 : c + 2] + got[:, c + 2 : c + 3]
+        c = (hd // 2) * i
+        m_col = stats[:, c : c + 1] + stats[:, c + 1 : c + 2] + stats[:, c + 2 : c + 3]
         m_row = jnp.sum(jnp.where(same, m_col, 0.0), axis=0, keepdims=True)
         peak = jnp.max(jnp.where(owns, m_row, NEG), axis=1, keepdims=True)
         weight = jnp.exp(jnp.where(owns, m_row - peak, NEG))
+        high = weight.astype(BF16).astype(F32)
+        weight = jnp.where(half, high, weight - high).astype(BF16)
+        block = jnp.concatenate([got[:, i * hd : (i + 1) * hd], stats], axis=1).astype(BF16)
+        mixed = jnp.dot(
+            weight, jnp.concatenate([block, block], axis=0), preferred_element_type=F32
+        )
+        c = hd + (hd // 2) * i + 3
         peaks.append(peak)
-        high = weight.astype(BF16).astype(F32)
-        weights += [high, weight - high]
-    mixed = jnp.dot(
-        jnp.concatenate(weights, axis=0).astype(BF16), got.astype(BF16),
-        preferred_element_type=F32,
-    )
-    wholes, outs = [], []
-    for i in range(2):
-        both = mixed[2 * i * R : (2 * i + 1) * R] + mixed[(2 * i + 1) * R : (2 * i + 2) * R]
-        c = 2 * hd + (hd // 2) * i + 3
-        wholes.append(both[:, c : c + 1] + both[:, c + 1 : c + 2] + both[:, c + 2 : c + 3])
-        outs.append(both[:, i * hd : (i + 1) * hd])
+        wholes.append(mixed[:, c : c + 1] + mixed[:, c + 1 : c + 2] + mixed[:, c + 2 : c + 3])
+        outs.append(mixed[:, :hd])
     mixed_stats = spread(peaks + wholes, iota((R, hd), 1), hd)
     packed = jnp.concatenate(outs + [mixed_stats], axis=1)
     per = R // G
@@ -259,11 +262,12 @@
     attn = jnp.concatenate(heads, axis=1)
     col = iota(attn.shape, 1)
     attn = jnp.where((col >= par * 64) & (col < par * 64 + wo_rows), attn, 0.0).astype(BF16)
-    part = jnp.dot(attn, wo[...], preferred_element_type=F32)
     width = precv.shape[2]
-    for t in range(T):
-        psend[t] = part[:, t * width : (t + 1) * width]
-    send_t(5, psend, precv, True)
+    for p in peers_t + [me_t]:
+        columns = pl.ds(pl.multiple_of(p * width, width), width)
+        psend[p] = jnp.dot(attn, wo[:, columns], preferred_element_type=F32)
+        if p is not me_t:
+            copy_t(5, psend.at[p], precv, p).start()
     cp_own = pltpu.make_async_copy(psend.at[me_t], precv.at[me_t], local_sem.at[6])
     cp_own.start()
     wait(recv_sem, 5, precv)
@@ -290,7 +294,7 @@
             functools.partial(kernel, G, T),
             name="decode",
             out_shape=jax.ShapeDtypeStruct((T, per, width), F32),
-            in_specs=[hbm] * 6,
+            in_specs=[pl.BlockSpec(memory_space=pltpu.HBM)] * 6,
             out_specs=hbm,
             scratch_shapes=[
                 pltpu.VMEM(hidden_in.shape, BF16),
@@ -311,8 +315,8 @@
                 pltpu.VMEM((T, per, width), F32),
                 dma((7,)), dma((6,)), dma((6,)),
             ],
-            compiler_params=pltpu.CompilerParams(collective_id=0, has_side_effects=True),
-        )(hidden_in, w_qkv, w_out, kv_pool, page_table.T, lengths.reshape(1, -1))
+            compiler_params=pltpu.CompilerParams(collective_id=0, has_side_effects=True, vmem_limit_bytes=12 * 2**20),
+        )(*[pltpu.with_memory_space_constraint(x, pltpu.HBM) for x in (hidden_in, w_qkv, w_out, kv_pool, page_table.T, lengths.reshape(1, -1))])
         return jnp.sum(parts, axis=0).astype(BF16)
 
     return jax.shard_map(

time: 36.5 us -> 35.5 us (0.973)
  other arithmetic: 1.32 us -> 0.58 us
    reduce_sum x1, other arithmetic: 1.32 us -> 0.58 us  [on_device(): return jnp.sum(parts, axis=0).astype(BF16)]
where the time goes in v4:
time: 35.5 us; the launch traced here: 35.4 us
  Pallas kernels  34.8 us (98%)
  other arithmetic  0.58 us (2%)
    pallas_call x1, Pallas kernels, on_device(): pl.pallas_call(functools.partial(kernel, G, T), name='decode', out_shape=...  34.8 us

profile of v4, /device:TPU:1, one launch (start us, length us, event | category | flops | bytes accessed | tf_op | source)
XLA Modules:
  0.0 35.4 jit_solution(7802957251216198910)
XLA Ops:
  0.0 34.8 %decode.1 = f32[8,2,384]{2,1,0:T(2,128)S(1)} custom-call(bf16[2,3072]{1,0:T(2,128)(2,1)} %hid_hbm.1, bf16[3072,256]{1,0:T(8,128)(2,1)} %wq_hbm.1, bf16[192,3072]{1,0:T(8,128)(2,1)} %wo_hbm.1, bf16[8,128,512]{2,1,0:T(8,128)(2,1)} %kv_hbm.1, s32[32,64]{1,0:T(8,128)} %bitcast.2, s32[1,64]{1,0:T(1,128)} %bitcast.3), custom_call_target="tpu_custom_call" | custom-call | tf_op jit(solution)/shard_map/decode/pallas_call | solution.py:293
  34.8 0.6 %reduce_sum.9 = bf16[2,384]{1,0:T(2,128)(2,1)} reduce(f32[8,2,384]{2,1,0:T(2,128)S(1)} %decode.1, f32[]{:T(128)} %constant.0.clone.1), dimensions={0}, to_apply=%region_0.0 | reduce | flops 5376 | bytes 26116 | tf_op jit(solution)/shard_map/reduce_sum | solution.py:320

commit v5 on v4

--- a/solution.py
+++ b/solution.py
@@ -29,13 +29,6 @@
     hops = lambda d: min(d, n - d)
     all_d = [(x, y, c) for x in range(n) for y in range(n) for c in range(2)]
     return sorted(all_d[1:], key=lambda o: -(hops(o[0]) + hops(o[1])) * 2 - o[2])
-
-
-def spread(columns, lane, width):
-    out = columns[-1]
-    for i in range(len(columns) - 2, -1, -1):
-        out = jnp.where(lane == i, columns[i], out)
-    return jnp.broadcast_to(out, (out.shape[0], width))
 
 
 def kernel(
@@ -65,10 +58,10 @@
     peers_t = [lax.rem(me_t + d, T) for d in order_t(T)]
 
     barrier = pltpu.get_barrier_semaphore()
+    for p in peers_g:
+        pl.semaphore_signal(barrier, inc=1, device_id=(p, me_t), device_id_type=MESH)
     for p in peers_t:
         pl.semaphore_signal(barrier, inc=1, device_id=(me_g, p), device_id_type=MESH)
-    for p in peers_g:
-        pl.semaphore_signal(barrier, inc=1, device_id=(p, me_t), device_id_type=MESH)
 
     wo_rows = wo_hbm.shape[0]
     wo_base = pl.multiple_of(par * 64, 64)
@@ -221,8 +214,11 @@
         peaks.append(peak)
         wholes.append(mixed[:, c : c + 1] + mixed[:, c + 1 : c + 2] + mixed[:, c + 2 : c + 3])
         outs.append(mixed[:, :hd])
-    mixed_stats = spread(peaks + wholes, iota((R, hd), 1), hd)
-    packed = jnp.concatenate(outs + [mixed_stats], axis=1)
+    even = lax.rem(iota((R, hd), 1), 2) == 0
+    packed = jnp.concatenate(
+        outs + [jnp.where(even, peaks[0], peaks[1]), jnp.where(even, wholes[0], wholes[1])],
+        axis=1,
+    )
     per = R // G
     for g in range(G):
         esend[g] = packed[g * per : (g + 1) * per, :]
@@ -244,21 +240,21 @@
         jnp.sum(own_head(first + i) * own_kv(6, first + i), axis=1, keepdims=True) * scale
         for i in range(2)
     ]
+    pick = lax.rem(iota((per, hd), 1), 2) == 0
+    own_score = jnp.where(pick, own_scores[0], own_scores[1])
     own_values = [own_kv(7, first + i) for i in range(2)]
     cp_wo.wait()
     wait(recv_sem, 4, erecv)
 
-    every = erecv[...]
+    m = erecv[:, :, 2 * hd : 3 * hd]
+    peak = jnp.maximum(jnp.max(m, axis=0), own_score)
+    f = jnp.exp(m - peak[None])
+    own_f = jnp.exp(own_score - peak)
+    whole = jnp.sum(f * erecv[:, :, 3 * hd : 4 * hd], axis=0) + own_f
     heads = []
     for i in range(2):
-        m = every[:, :, 2 * hd + i : 2 * hd + i + 1]
-        l = every[:, :, 2 * hd + 2 + i : 2 * hd + 3 + i]
-        peak = jnp.maximum(jnp.max(m, axis=0), own_scores[i])
-        f = jnp.exp(m - peak[None])
-        own_f = jnp.exp(own_scores[i] - peak)
-        whole = jnp.sum(f * l, axis=0) + own_f
-        summed = jnp.sum(f * every[:, :, i * hd : (i + 1) * hd], axis=0) + own_f * own_values[i]
-        heads.append(summed / whole)
+        summed = jnp.sum(f[:, :, i : i + 1] * erecv[:, :, i * hd : (i + 1) * hd], axis=0)
+        heads.append((summed + own_f[:, i : i + 1] * own_values[i]) / whole[:, i : i + 1])
     attn = jnp.concatenate(heads, axis=1)
     col = iota(attn.shape, 1)
     attn = jnp.where((col >= par * 64) & (col < par * 64 + wo_rows), attn, 0.0).astype(BF16)
@@ -310,8 +306,8 @@
                 pltpu.VMEM((T, slots, cols), BF16),
                 pltpu.VMEM((T, slots, wide), BF16),
                 pltpu.VMEM((T, slots, wide), BF16),
-                pltpu.VMEM((G, per, wide), F32),
-                pltpu.VMEM((G, per, wide), F32),
+                pltpu.VMEM((G, per, wide + HEAD_DIM), F32),
+                pltpu.VMEM((G, per, wide + HEAD_DIM), F32),
                 pltpu.VMEM((T, per, width), F32),
                 dma((7,)), dma((6,)), dma((6,)),
             ],

time: 35.5 us -> 35.4 us (level)
  no operation moved by 1% of the time
where the time goes in v5:
time: 35.4 us; the launch traced here: 35.3 us
  Pallas kernels  34.7 us (98%)
  other arithmetic  0.58 us (2%)
    pallas_call x1, Pallas kernels, on_device(): pl.pallas_call(functools.partial(kernel, G, T), name='decode', out_shape=...  34.7 us

profile of v5, /device:TPU:1, one launch (start us, length us, event | category | flops | bytes accessed | tf_op | source)
XLA Modules:
  0.0 35.3 jit_solution(3799732687375298666)
XLA Ops:
  0.0 34.7 %decode.1 = f32[8,2,384]{2,1,0:T(2,128)S(1)} custom-call(bf16[2,3072]{1,0:T(2,128)(2,1)} %hid_hbm.1, bf16[3072,256]{1,0:T(8,128)(2,1)} %wq_hbm.1, bf16[192,3072]{1,0:T(8,128)(2,1)} %wo_hbm.1, bf16[8,128,512]{2,1,0:T(8,128)(2,1)} %kv_hbm.1, s32[32,64]{1,0:T(8,128)} %bitcast.2, s32[1,64]{1,0:T(1,128)} %bitcast.3), custom_call_target="tpu_custom_call" | custom-call | tf_op jit(solution)/shard_map/decode/pallas_call | solution.py:289
  34.7 0.6 %reduce_sum.9 = bf16[2,384]{1,0:T(2,128)(2,1)} reduce(f32[8,2,384]{2,1,0:T(2,128)S(1)} %decode.1, f32[]{:T(128)} %constant.0.clone.1), dimensions={0}, to_apply=%region_0.0 | reduce | flops 5376 | bytes 26116 | tf_op jit(solution)/shard_map/reduce_sum | solution.py:316
